TPU v7x, 32 devices: a whole 2x2x4 slice. The times are simulated.
32 devices in a mesh: space: 8 (over z, y), slab: 4 (over x, core).
Axes of the slice: x: 2, y: 2, z: 4, core: 2. Of those that a mesh axis runs over, the one named last changes fastest.
Arguments:
- features: float32 [128, 8, 8, 512], P(('space', 'slab')), may hold values from -6 to 6
- live: int32 [32], P(('space', 'slab')), may hold values from 1 to 4, as said below
- rim_slots: int32 [32, 2], P(('space', 'slab')), may hold values from 0 to 3, as said below
- neighbours: int32 [128, 26], P(('space', 'slab')), may hold values from 0 to 12, as said below
- weights: float32 [4, 27, 4096], replicated, may hold values from -0.15625 to 0.15625
- biases: float32 [4, 64], replicated, may hold values from -3 to 3
Outputs:
- output: float32 [128, 8, 8, 512], P(('space', 'slab'))
Inputs may be any that keep to these rules, and one draw needn't show every extreme that they name: `live`: devices whose space indices differ by 8 / 2 (same slab index) hold at most 6 occupied bricks together; in every draw some pair holds exactly that and some device holds 4. `rim_slots`: every entry is below its device's live count. `neighbours`: entries below 4 are below the device's live count.
All inputs are finite; a program needn't handle non-finite values.
Results may differ from a plain program's by a relative error of at most 0.0003.
Values sent between devices are 32-bit elements; how exact they have to be, the bound alone decides.
A program may use at most 128 MiB of HBM per device.

v0:
```python
import functools

import jax
import jax.numpy as jnp
from jax import lax
from jax.experimental import pallas as pl
from jax.experimental.pallas import tpu as pltpu
from jax.sharding import PartitionSpec as P

MESH = pl.DeviceIdType.MESH
SIDE = 8


def direction_number(dx, dy, dz):
    index = 9 * (dx + 1) + 3 * (dy + 1) + (dz + 1)
    return index if index < 13 else index - 1


def layers_kernel(
    nsp, nsl, nbr, live, rim, feat, bias, w_hbm, out,
    cur, hid, own, offer, pad, cols, whi, wlo, wbuf, acc,
    wsem, ssem, rsem, *tabs,
):
    bricks = feat.shape[0]
    width = feat.shape[-1]
    ch = width // SIDE
    half = width // 2
    pair = 2 * ch
    ktile = half + pair
    kdy = 3 * ktile
    rims = offer.shape[1]
    convs = w_hbm.shape[1]
    sp = lax.axis_index("space")
    sl = lax.axis_index("slab")
    peers = (
        (sp > 0, (sp - 1, sl)),
        (sp < nsp - 1, (sp + 1, sl)),
        (sl > 0, (sp, sl - 1)),
        (sl < nsl - 1, (sp, sl + 1)),
    )

    barrier = pltpu.get_barrier_semaphore()
    for has, peer in peers:
        @pl.when(has)
        def _():
            pl.semaphore_signal(barrier, inc=1, device_id=peer, device_id_type=MESH)

    def weight_copy(k):
        return pltpu.make_async_copy(w_hbm.at[:, k], wbuf.at[k], wsem.at[k])

    for k in range(convs):
        weight_copy(k).start()

    def remote(k, d):
        first = bricks + rims * (d ^ 1)
        return pltpu.make_async_remote_copy(
            src_ref=offer.at[k],
            dst_ref=tabs[k].at[pl.ds(first, rims)],
            send_sem=ssem.at[k, d],
            recv_sem=rsem.at[k, d ^ 1],
            device_id=peers[d][1],
            device_id_type=MESH,
        )

    def mask_of(b):
        return jnp.where(b < live[0], 1.0, 0.0).astype(jnp.float32)

    low = lax.broadcasted_iota(jnp.int32, (SIDE, pair), 1) < ch
    low1 = lax.broadcasted_iota(jnp.int32, (1, pair), 1) < ch

    def take_faces(src, k):
        def one(b, carry):
            own[b, 0] = src[b, 0]
            own[b, 1] = src[b, SIDE - 1]
            for s, y in ((2, 0), (3, SIDE - 1)):
                for x in range(SIDE):
                    own[b, s, x:x + 1, :] = src[b, x, y:y + 1, :]
            for x in range(SIDE):
                at = (x % 4) * pair
                own[b, 4 + x // 4, :, at:at + pair] = jnp.where(
                    low, src[b, x, :, 0:pair], src[b, x, :, width - pair:width]
                )
            tabs[k][b] = own[b]
            return carry

        lax.fori_loop(0, bricks, one, 0)
        for r in range(rims):
            offer[k, r] = own[rim[0, r]]

    def send(k):
        for d in range(4):
            @pl.when(peers[d][0])
            def _():
                remote(k, d).start()

    def receive(k):
        for d in range(4):
            @pl.when(peers[d][0])
            def _():
                remote(k, d ^ 1).wait_recv()

    def finish_sends(k):
        for d in range(4):
            @pl.when(peers[d][0])
            def _():
                remote(k, d).wait_send()

    def build_weights(k):
        weight_copy(k).wait()

        def one(t, carry):
            a = t // 3
            base = pl.multiple_of((t - 3 * a) * ktile, ktile)
            taps = [wbuf[k, 3 * t + i] for i in range(3)]
            none = jnp.zeros((ch, ch), jnp.float32)
            for j in range(4):
                block = jnp.concatenate(
                    [taps[j] if j < 3 else none, taps[j - 1] if j > 0 else none], axis=1
                )
                hi = block.astype(jnp.bfloat16)
                lo = (block - hi.astype(jnp.float32)).astype(jnp.bfloat16)
                for q in range(2):
                    z = j - 1 + 2 * q
                    row = base + (z if z >= 0 else 5) * ch
                    row = pl.multiple_of(row, ch)
                    lanes = slice(q * pair, (q + 1) * pair)
                    whi[a, pl.ds(row, ch), lanes] = hi
                    whi[a, pl.ds(pl.multiple_of(row + kdy, ch), ch), lanes] = hi
                    wlo[a, pl.ds(row, ch), lanes] = lo
            return carry

        lax.fori_loop(0, 9, one, 0)

    def row_of(center, below, above, mask):
        return jnp.concatenate(
            [
                center[:, :half],
                jnp.where(mask, center[:, half:half + pair], below),
                center[:, half:],
                jnp.where(mask, above, center[:, half - pair:half]),
            ],
            axis=1,
        )

    def build_columns(src, k):
        tab = tabs[k]

        def one(b, carry):
            def entry(dx, dy, dz):
                return nbr[b, direction_number(dx, dy, dz)]

            for dx, xrow, s in ((-1, 0, 1), (1, SIDE + 1, 0)):
                pad[xrow, 1:SIDE + 1, :] = row_of(
                    tab[entry(dx, 0, 0), s],
                    tab[entry(dx, 0, -1), s, :, width - pair:width],
                    tab[entry(dx, 0, 1), s, :, 0:pair],
                    low,
                )
                for dy, yrow, y in ((-1, 0, SIDE - 1), (1, SIDE + 1, 0)):
                    pad[xrow, yrow:yrow + 1, :] = row_of(
                        tab[entry(dx, dy, 0), s, y:y + 1, :],
                        tab[entry(dx, dy, -1), s, y:y + 1, width - pair:width],
                        tab[entry(dx, dy, 1), s, y:y + 1, 0:pair],
                        low1,
                    )
            nlow, nhigh = entry(0, 0, -1), entry(0, 0, 1)
            for x in range(SIDE):
                at = (x % 4) * pair
                pad[1 + x, 1:SIDE + 1, :] = row_of(
                    src[b, x],
                    tab[nlow, 4 + x // 4, :, at:at + pair],
                    tab[nhigh, 4 + x // 4, :, at:at + pair],
                    low,
                )
            for dy, yrow, s in ((-1, 0, 3), (1, SIDE + 1, 2)):
                rows = row_of(
                    tab[entry(0, dy, 0), s],
                    tab[entry(0, dy, -1), s, :, width - pair:width],
                    tab[entry(0, dy, 1), s, :, 0:pair],
                    low,
                )
                for x in range(SIDE):
                    pad[1 + x, yrow:yrow + 1, :] = rows[x:x + 1]
            at = pl.multiple_of(b * 2 * SIDE, 2 * SIDE)
            for x in range(SIDE + 2):
                for dy in range(3):
                    v = pad[x, dy:dy + SIDE, :]
                    v = jnp.concatenate([v[:, :ktile], v[:, ktile:]], axis=0)
                    hi = v.astype(jnp.bfloat16)
                    lo = (v - hi.astype(jnp.float32)).astype(jnp.bfloat16)
                    cols[x, pl.ds(at, 2 * SIDE), dy * ktile:(dy + 1) * ktile] = hi
                    cols[x, pl.ds(at, 2 * SIDE), kdy + dy * ktile:kdy + (dy + 1) * ktile] = lo
            return carry

        lax.fori_loop(0, bricks, one, 0)

    def convolve():
        rows = SIDE * bricks * 2 * SIDE
        total = None
        for a in range(3):
            left = cols[a:a + SIDE].reshape(rows, 2 * kdy)
            term = jnp.dot(left, whi[a], preferred_element_type=jnp.float32)
            total = term if total is None else total + term
            left = cols[a:a + SIDE, :, :kdy].reshape(rows, kdy)
            total = total + jnp.dot(left, wlo[a], preferred_element_type=jnp.float32)
        acc[...] = total.reshape(acc.shape)

    def epilogue(k, res, dst):
        bvec = bias[k:k + 1, :]
        bvec = jnp.concatenate([bvec, bvec, bvec, bvec], axis=1)

        def one(b, carry):
            m = mask_of(b)
            for x in range(SIDE):
                for t in range(2):
                    at = pl.multiple_of(b * 2 * SIDE + t * SIDE, SIDE)
                    v = acc[x, pl.ds(at, SIDE), :] + bvec
                    lanes = slice(t * half, (t + 1) * half)
                    if res is not None:
                        v = v + res[b, x, :, lanes]
                    dst[b, x, :, lanes] = jnp.maximum(v, 0.0) * m
            return carry

        lax.fori_loop(0, bricks, one, 0)

    def mask_features(b, carry):
        cur[b] = feat[b] * mask_of(b)
        return carry

    lax.fori_loop(0, bricks, mask_features, 0)
    take_faces(cur, 0)
    arrivals = sum(jnp.where(has, 1, 0) for has, _ in peers)
    pl.semaphore_wait(barrier, arrivals)
    send(0)

    whi[...] = jnp.zeros_like(whi)
    wlo[...] = jnp.zeros_like(wlo)
    last = bricks + 4 * rims
    for k in range(convs):
        tabs[k][last] = jnp.zeros(tabs[k].shape[1:], jnp.float32)
    for d in range(4):
        @pl.when(jnp.logical_not(peers[d][0]))
        def _():
            for k in range(convs):
                for r in range(rims):
                    tabs[k][bricks + rims * d + r] = jnp.zeros(tabs[k].shape[1:], jnp.float32)

    for k in range(convs):
        src = cur if k % 2 == 0 else hid
        if k % 2 == 0:
            dst = hid
        else:
            dst = cur if k < convs - 1 else out
        build_weights(k)
        receive(k)
        build_columns(src, k)
        convolve()
        epilogue(k, None if k % 2 == 0 else cur, dst)
        if k < convs - 1:
            take_faces(dst, k + 1)
            send(k + 1)
    for k in range(convs):
        finish_sends(k)


def shards(nsp, nsl, features, live, rim_slots, neighbours, weights, biases):
    bricks, _, _, width = features.shape
    ch = biases.shape[-1]
    convs = weights.shape[0]
    rims = rim_slots.shape[-1]
    entries = bricks + 4 * rims + 1
    taps = weights.transpose(1, 0, 2).reshape(weights.shape[1], convs, ch, ch)
    half = width // 2
    kdy = 3 * (half + 2 * ch)
    f32, bf16 = jnp.float32, jnp.bfloat16
    smem = pl.BlockSpec(memory_space=pltpu.SMEM)
    vmem = pl.BlockSpec(memory_space=pltpu.VMEM)
    return pl.pallas_call(
        functools.partial(layers_kernel, nsp, nsl),
        out_shape=jax.ShapeDtypeStruct(features.shape, f32),
        in_specs=[smem, smem, smem, vmem, vmem, pl.BlockSpec(memory_space=pl.ANY)],
        out_specs=vmem,
        scratch_shapes=[
            pltpu.VMEM(features.shape, f32),
            pltpu.VMEM(features.shape, f32),
            pltpu.VMEM((bricks, 6, SIDE, width), f32),
            pltpu.VMEM((convs, rims, 6, SIDE, width), f32),
            pltpu.VMEM((SIDE + 2, 2 * SIDE, width + 4 * ch), f32),
            pltpu.VMEM((SIDE + 2, bricks * 2 * SIDE, 2 * kdy), bf16),
            pltpu.VMEM((3, 2 * kdy, half), bf16),
            pltpu.VMEM((3, kdy, half), bf16),
            pltpu.VMEM((convs, weights.shape[1], ch, ch), f32),
            pltpu.VMEM((SIDE, bricks * 2 * SIDE, half), f32),
            pltpu.SemaphoreType.DMA((convs,)),
            pltpu.SemaphoreType.DMA((convs, 4)),
            pltpu.SemaphoreType.DMA((convs, 4)),
        ]
        + [pltpu.VMEM((entries, 6, SIDE, width), f32) for _ in range(convs)],
        compiler_params=pltpu.CompilerParams(
            collective_id=0, has_side_effects=True, vmem_limit_bytes=56 * 1024 * 1024
        ),
        name="layers",
    )(neighbours, live, rim_slots, features, biases, taps)


def solution(mesh):
    in_specs = (
        P(("space", "slab"), None, None, None),
        P(("space", "slab")),
        P(("space", "slab"), None),
        P(("space", "slab"), None),
        P(),
        P(),
    )
    out_specs = P(("space", "slab"), None, None, None)
    body = functools.partial(shards, mesh.shape["space"], mesh.shape["slab"])
    return jax.shard_map(body, mesh=mesh, in_specs=in_specs, out_specs=out_specs, check_vma=False)
```

profile of v0, /device:TPU:12, one launch (start us, length us, event | category | flops | bytes accessed | tf_op | source)
XLA Modules:
  0.0 75.0 jit_solution(16795077434405720776)
XLA Ops:
  0.7 4.2 %reshape.3.w_hbm = f32[27,4,64,64]{3,2,1,0:T(8,128)} reshape(f32[27,4,4096]{2,1,0:T(4,128)} %bitcast.1) | data formatting | bytes 3538944 | tf_op jit(solution)/shard_map/reshape | solution.py:272
  4.8 68.3 %layers.1 = f32[4,8,8,512]{3,2,1,0:T(8,128)} custom-call(s32[4,26]{1,0:T(4,128)} %nbr.1, s32[1]{0:T(128)S(6)} %copy.8.live, s32[1,2]{1,0:T(1,128)} %rim.1, f32[4,8,8,512]{3,2,1,0:T(8,128)} %feat.1, f32[4,64]{1,0:T(4,128)} %bias.1, f32[27,4,64,64]{3,2,1,0:T(8,128)} %reshape.3.w_hbm), custom_call_target="tpu_custom_call" | custom-call | tf_op jit(solution)/shard_map/layers/pallas_call | solution.py:278
  73.1 1.9 %copy.9 = f32[4,8,8,512]{3,2,1,0:T(8,128)} copy(f32[4,8,8,512]{3,2,1,0:T(8,128)} %layers.1) | data formatting | bytes 1048576
where the time goes:
time: 75.2 us; the launch traced here: 75 us
  Pallas kernels  68.3 us (91%)
  local copies, waits for them, and re-layouts  6.04 us (8%)
    pallas_call x1, Pallas kernels, shards(): pl.pallas_call(functools.partial(layers_kernel, nsp, nsl), out_shape=jax....  68.3 us
    reshape x1, local copies, waits for them, and re-layouts, shards(): taps = weights.transpose(1, 0, 2).reshape(weights.shape[1], convs, ch, ch)  4.18 us
    unnamed x1, local copies, waits for them, and re-layouts  1.87 us

commit v1 on v0

v1 whole, which is shorter than its diff:
```python
import functools

import jax
import jax.numpy as jnp
from jax import lax
from jax.experimental import pallas as pl
from jax.experimental.pallas import tpu as pltpu
from jax.sharding import PartitionSpec as P

MESH = pl.DeviceIdType.MESH
SIDE = 8
RELAYED = 4


def direction_number(dx, dy, dz):
    index = 9 * (dx + 1) + 3 * (dy + 1) + (dz + 1)
    return index if index < 13 else index - 1


def layers_kernel(
    nsp, nsl, nbr, live, rim, feat, bias, w_hbm, out,
    cur, hid, offx, offy, offz, pad, cols, whi, wlo, wbuf, blk, acc,
    emap, inv, perm, nb, wsem, ssem, rsem, *tabs,
):
    bricks = feat.shape[0]
    width = feat.shape[-1]
    ch = width // SIDE
    half = width // 2
    pair = 2 * ch
    ktile = half + pair
    kdy = 3 * ktile
    rims = offx.shape[1]
    convs = w_hbm.shape[2]
    tabx, taby, tabz = tabs[:convs], tabs[convs:2 * convs], tabs[2 * convs:]
    last = bricks + 4 * rims
    sp = lax.axis_index("space")
    sl = lax.axis_index("slab")
    odd = lax.rem(sp, 2)

    near = (sp + 1 - 2 * odd, sl)
    far = (sp - 1 + 2 * odd, sl)
    via = (sp - 2 + 4 * odd, sl)
    onto = (sp + 2 - 4 * odd, sl)
    has_far = jnp.where(odd == 1, sp < nsp - 1, sp > 0)
    has_onto = jnp.where(odd == 1, sp > 1, sp < nsp - 2)
    lower = (sl > 0, (sp, sl - 1))
    upper = (sl < nsl - 1, (sp, sl + 1))
    near_first = bricks + rims * (1 - odd)
    far_first = bricks + rims * odd

    barrier = pltpu.get_barrier_semaphore()
    greeted = ((sp >= 0, near), (has_far, far), (has_far, via), (has_onto, onto), lower, upper)
    for has, peer in greeted:
        @pl.when(has)
        def _():
            pl.semaphore_signal(barrier, inc=1, device_id=peer, device_id_type=MESH)

    def weight_copy(k):
        return pltpu.make_async_copy(w_hbm.at[:, :, k], wbuf.at[k], wsem.at[k])

    for k in range(convs):
        weight_copy(k).start()

    chunks = [(j, part) for j in range(rims) for part in range(3)]
    relayed = min(RELAYED, len(chunks))

    def offered(k, j, part):
        if part == 0:
            return offx.at[k, j]
        if part == 1:
            return offy.at[k, j, :, 1:SIDE - 1, :]
        return offz.at[k, j]

    def entry_of(k, at, part):
        if part == 0:
            return tabx[k].at[at]
        if part == 1:
            return taby[k].at[at, :, 1:SIDE - 1, :]
        return tabz[k].at[at]

    def copy(k, src, dst, flow, index, peer):
        return pltpu.make_async_remote_copy(
            src_ref=src, dst_ref=dst, send_sem=ssem.at[k, flow, index],
            recv_sem=rsem.at[k, flow, index], device_id=peer, device_id_type=MESH,
        )

    def to_near(k, c):
        j, part = chunks[c]
        return copy(k, offered(k, j, part), entry_of(k, far_first + j, part), 0, c, near)

    def from_near(k, c):
        j, part = chunks[c]
        return copy(k, offered(k, j, part), entry_of(k, near_first + j, part), 0, c, near)

    def to_far(k, c):
        j, part = chunks[c]
        return copy(k, offered(k, j, part), entry_of(k, near_first + j, part), 1, c, far)

    def relay(k, c):
        j, part = chunks[c]
        return copy(
            k, entry_of(k, near_first + j, part), entry_of(k, far_first + j, part), 1, c, onto
        )

    def from_far(k, c):
        j, part = chunks[c]
        return copy(k, offered(k, j, part), entry_of(k, far_first + j, part), 1, c, far)

    def beside(k, d, j, part, to):
        first = bricks + rims * (d ^ 1 if to else d)
        index = 3 * j + part
        peer = (lower if d == 2 else upper)[1]
        return pltpu.make_async_remote_copy(
            src_ref=offered(k, j, part), dst_ref=entry_of(k, first + j, part),
            send_sem=ssem.at[k, d, index], recv_sem=rsem.at[k, d ^ 1 if to else d, index],
            device_id=peer, device_id_type=MESH,
        )

    def send(k):
        for c in range(relayed):
            to_near(k, c).start()
        for c in range(relayed, len(chunks)):
            to_near(k, c).start()

            @pl.when(has_far)
            def _():
                to_far(k, c).start()
        for d, (has, _) in ((2, lower), (3, upper)):
            @pl.when(has)
            def _():
                for j, part in chunks:
                    beside(k, d, j, part, True).start()

    def pass_on(k, some):
        for c in some:
            from_near(k, c).wait_recv()

            @pl.when(has_onto)
            def _():
                relay(k, c).start()

    def receive(k):
        for c in range(relayed, len(chunks)):
            from_near(k, c).wait_recv()
        for d, (has, _) in ((2, lower), (3, upper)):
            @pl.when(has)
            def _():
                for j, part in chunks:
                    beside(k, d, j, part, False).wait_recv()

        @pl.when(has_far)
        def _():
            for c in range(len(chunks)):
                from_far(k, c).wait_recv()

    def finish_sends(k):
        for c in range(len(chunks)):
            to_near(k, c).wait_send()

        @pl.when(has_far)
        def _():
            for c in range(relayed, len(chunks)):
                to_far(k, c).wait_send()

        @pl.when(has_onto)
        def _():
            for c in range(relayed):
                relay(k, c).wait_send()
        for d, (has, _) in ((2, lower), (3, upper)):
            @pl.when(has)
            def _():
                for j, part in chunks:
                    beside(k, d, j, part, True).wait_send()

    slots = [rim[0, j] for j in range(rims)]
    score = []
    for b in range(bricks):
        s = rims + b
        for j in reversed(range(rims)):
            s = jnp.where(slots[j] == b, j, s)
        score.append(s)
    place = [
        sum(jnp.where(score[o] < score[b], 1, 0) for o in range(bricks) if o != b)
        for b in range(bricks)
    ]
    held = [
        sum(jnp.where(place[b] == p, b, 0) for b in range(bricks)) for p in range(bricks)
    ]
    for b in range(bricks):
        inv[b] = place[b]
        perm[b] = held[b]
    spot = [sum(jnp.where(slots[j] == b, place[b], 0) for b in range(bricks)) for j in range(rims)]

    def mask_of(b):
        return jnp.where(b < live[0], 1.0, 0.0).astype(jnp.float32)

    low = lax.broadcasted_iota(jnp.int32, (SIDE, pair), 1) < ch
    low1 = lax.broadcasted_iota(jnp.int32, (1, pair), 1) < ch
    loww = lax.broadcasted_iota(jnp.int32, wbuf.shape[2:], 1) < ch

    def take_faces(src, k, group):
        def one(p, carry):
            tabx[k][p, 0] = src[p, 0]
            tabx[k][p, 1] = src[p, SIDE - 1]
            for s, y in ((0, 0), (1, SIDE - 1)):
                for x in range(1, SIDE - 1):
                    taby[k][p, s, x:x + 1, :] = src[p, x, y:y + 1, :]
            for x in range(1, SIDE - 1):
                at = (x - 1) * pair
                tabz[k][p, :, at:at + pair] = jnp.where(
                    low, src[p, x, :, 0:pair], src[p, x, :, width - pair:width]
                )
            return carry

        lax.fori_loop(group[0], group[1], one, 0)

    def make_offer(k):
        for j in range(rims):
            for off, tab in ((offx, tabx[k]), (offy, taby[k]), (offz, tabz[k])):
                value = tab[0]
                for p in range(1, j + 1):
                    value = jnp.where(spot[j] == p, tab[p], value)
                off[k, j] = value

    def build_weights(k):
        weight_copy(k).wait()

        def one(t, carry):
            a = t // 3
            base = pl.multiple_of((t - 3 * a) * ktile, ktile)
            taps = [wbuf[k, 3 * t + i] for i in range(3)]
            turned = [pltpu.roll(tap, ch, 1) for tap in taps]
            none = jnp.zeros(taps[0].shape, jnp.float32)
            rows = taps[0].shape[0]
            for j in range(4):
                first, first_turned = (taps[j], turned[j]) if j < 3 else (none, none)
                second, second_turned = (taps[j - 1], turned[j - 1]) if j > 0 else (none, none)
                blk[j, pl.ds(0, rows, stride=2), :] = jnp.where(loww, first, second_turned)
                blk[j, pl.ds(1, rows, stride=2), :] = jnp.where(loww, first_turned, second)
            for j in range(4):
                block = blk[j]
                hi = block.astype(jnp.bfloat16)
                lo = (block - hi.astype(jnp.float32)).astype(jnp.bfloat16)
                for q in range(2):
                    z = j - 1 + 2 * q
                    row = base + (z if z >= 0 else 5) * ch
                    row = pl.multiple_of(row, ch)
                    lanes = slice(q * pair, (q + 1) * pair)
                    whi[a, pl.ds(row, ch), lanes] = hi
                    whi[a, pl.ds(pl.multiple_of(row + kdy, ch), ch), lanes] = hi
                    wlo[a, pl.ds(row, ch), lanes] = lo
            return carry

        lax.fori_loop(0, 9, one, 0)

    def row_of(center, below, above, mask):
        return jnp.concatenate(
            [
                center[:, :half],
                jnp.where(mask, center[:, half:half + pair], below),
                center[:, half:],
                jnp.where(mask, above, center[:, half - pair:half]),
            ],
            axis=1,
        )

    def build_columns(src, k, group, at_of):
        tx, ty, tz = tabx[k], taby[k], tabz[k]

        def one(i, carry):
            p = at_of(group[0] + i)

            def entry(dx, dy, dz):
                return nb[p, direction_number(dx, dy, dz)]

            def x_row(dx, dy, s, y):
                return row_of(
                    tx[entry(dx, dy, 0), s, y:y + 1, :],
                    tx[entry(dx, dy, -1), s, y:y + 1, width - pair:width],
                    tx[entry(dx, dy, 1), s, y:y + 1, 0:pair],
                    low1,
                )

            for dx, xrow, s in ((-1, 0, 1), (1, SIDE + 1, 0)):
                pad[xrow, 1:SIDE + 1, :] = row_of(
                    tx[entry(dx, 0, 0), s],
                    tx[entry(dx, 0, -1), s, :, width - pair:width],
                    tx[entry(dx, 0, 1), s, :, 0:pair],
                    low,
                )
                for dy, yrow, y in ((-1, 0, SIDE - 1), (1, SIDE + 1, 0)):
                    pad[xrow, yrow:yrow + 1, :] = x_row(dx, dy, s, y)
            nlow, nhigh = entry(0, 0, -1), entry(0, 0, 1)
            for x in range(SIDE):
                if x in (0, SIDE - 1):
                    s = 0 if x == 0 else 1
                    below = tx[nlow, s, :, width - pair:width]
                    above = tx[nhigh, s, :, 0:pair]
                else:
                    at = (x - 1) * pair
                    below = tz[nlow, :, at:at + pair]
                    above = tz[nhigh, :, at:at + pair]
                pad[1 + x, 1:SIDE + 1, :] = row_of(src[p, x], below, above, low)
            for dy, yrow, s, y in ((-1, 0, 1, SIDE - 1), (1, SIDE + 1, 0, 0)):
                rows = row_of(
                    ty[entry(0, dy, 0), s],
                    ty[entry(0, dy, -1), s, :, width - pair:width],
                    ty[entry(0, dy, 1), s, :, 0:pair],
                    low,
                )
                for x in range(1, SIDE - 1):
                    pad[1 + x, yrow:yrow + 1, :] = rows[x:x + 1]
                pad[1, yrow:yrow + 1, :] = x_row(0, dy, 0, y)
                pad[SIDE, yrow:yrow + 1, :] = x_row(0, dy, 1, y)
            at = pl.multiple_of(i * 2 * SIDE, 2 * SIDE)
            for x in range(SIDE + 2):
                for dy in range(3):
                    v = pad[x, dy:dy + SIDE, :]
                    v = jnp.concatenate([v[:, :ktile], v[:, ktile:]], axis=0)
                    hi = v.astype(jnp.bfloat16)
                    lo = (v - hi.astype(jnp.float32)).astype(jnp.bfloat16)
                    cols[x, pl.ds(at, 2 * SIDE), dy * ktile:(dy + 1) * ktile] = hi
                    cols[x, pl.ds(at, 2 * SIDE), kdy + dy * ktile:kdy + (dy + 1) * ktile] = lo
            return carry

        lax.fori_loop(0, group[1] - group[0], one, 0)

    def convolve(group):
        tall = (group[1] - group[0]) * 2 * SIDE
        steps = SIDE // 2
        totals = [None, None]
        for a in range(3):
            for h in range(2):
                x = a + h * steps
                left = cols[x:x + steps, :tall].reshape(steps * tall, 2 * kdy)
                term = jnp.dot(left, whi[a], preferred_element_type=jnp.float32)
                totals[h] = term if totals[h] is None else totals[h] + term
                left = cols[x:x + steps, :tall, :kdy].reshape(steps * tall, kdy)
                totals[h] = totals[h] + jnp.dot(left, wlo[a], preferred_element_type=jnp.float32)
        for h in range(2):
            acc[h * steps:(h + 1) * steps, :tall] = totals[h].reshape(steps, tall, half)

    def epilogue(k, res, dst, group, at_of):
        bvec = bias[k:k + 1, :]
        bvec = jnp.concatenate([bvec, bvec, bvec, bvec], axis=1)

        def one(i, carry):
            b = group[0] + i
            p = at_of(b)
            m = mask_of(perm[p])
            for x in range(SIDE):
                for t in range(2):
                    at = pl.multiple_of(i * 2 * SIDE + t * SIDE, SIDE)
                    v = acc[x, pl.ds(at, SIDE), :] + bvec
                    lanes = slice(t * half, (t + 1) * half)
                    if res is not None:
                        v = v + res[p, x, :, lanes]
                    dst[b, x, :, lanes] = jnp.maximum(v, 0.0) * m
            return carry

        lax.fori_loop(0, group[1] - group[0], one, 0)

    def mask_features(p, carry):
        cur[p] = feat[perm[p]] * mask_of(perm[p])
        return carry

    first = (0, rims)
    rest = (rims, bricks)
    lax.fori_loop(0, bricks, mask_features, 0)
    take_faces(cur, 0, first)
    make_offer(0)
    arrivals = sum(jnp.where(has, 1, 0) for has, _ in greeted)
    pl.semaphore_wait(barrier, arrivals)
    send(0)

    take_faces(cur, 0, rest)
    for k in range(convs):
        for tab in (tabx[k], taby[k], tabz[k]):
            tab[last] = jnp.zeros(tab.shape[1:], jnp.float32)
    for e in range(last + 1):
        if e < bricks:
            emap[e] = place[e]
        elif e < bricks + rims:
            emap[e] = jnp.where(sp > 0, e, last)
        elif e < bricks + 2 * rims:
            emap[e] = jnp.where(sp < nsp - 1, e, last)
        elif e < bricks + 3 * rims:
            emap[e] = jnp.where(sl > 0, e, last)
        elif e < last:
            emap[e] = jnp.where(sl < nsl - 1, e, last)
        else:
            emap[e] = last

    def remap(j, carry):
        for p in range(bricks):
            nb[p, j] = emap[nbr[perm[p], j]]
        return carry

    lax.fori_loop(0, nbr.shape[1], remap, 0)
    whi[...] = jnp.zeros_like(whi)
    wlo[...] = jnp.zeros_like(wlo)
    build_weights(0)
    pass_on(0, range(relayed))

    for k in range(convs):
        src = cur if k % 2 == 0 else hid
        res = None if k % 2 == 0 else cur
        receive(k)
        if k < convs - 1:
            dst = hid if k % 2 == 0 else cur
            for group in (first, rest):
                build_columns(src, k, group, lambda b: b)
                convolve(group)
                epilogue(k, res, dst, group, lambda b: b)
                take_faces(dst, k + 1, group)
                if group is first:
                    make_offer(k + 1)
                    send(k + 1)
            pass_on(k + 1, range(relayed - 2))
            build_weights(k + 1)
            pass_on(k + 1, range(relayed - 2, relayed))
        else:
            for group in (first, rest):
                build_columns(src, k, group, lambda b: inv[b])
                convolve(group)
                epilogue(k, res, out, group, lambda b: inv[b])
    for k in range(convs):
        finish_sends(k)


def shards(nsp, nsl, features, live, rim_slots, neighbours, weights, biases):
    bricks, _, _, width = features.shape
    ch = biases.shape[-1]
    convs, taps, _ = weights.shape
    rims = rim_slots.shape[-1]
    entries = bricks + 4 * rims + 1
    pair = 2 * ch
    rows = ch * ch // pair
    planes = weights.reshape(convs, taps, rows, pair).transpose(1, 2, 0, 3)
    half = width // 2
    kdy = 3 * (half + pair)
    group = max(rims, bricks - rims)
    inner = (SIDE - 2) * pair
    f32, bf16 = jnp.float32, jnp.bfloat16
    smem = pl.BlockSpec(memory_space=pltpu.SMEM)
    vmem = pl.BlockSpec(memory_space=pltpu.VMEM)
    return pl.pallas_call(
        functools.partial(layers_kernel, nsp, nsl),
        out_shape=jax.ShapeDtypeStruct(features.shape, f32),
        in_specs=[smem, smem, smem, vmem, vmem, pl.BlockSpec(memory_space=pl.ANY)],
        out_specs=vmem,
        scratch_shapes=[
            pltpu.VMEM(features.shape, f32),
            pltpu.VMEM(features.shape, f32),
            pltpu.VMEM((convs, rims, 2, SIDE, width), f32),
            pltpu.VMEM((convs, rims, 2, SIDE, width), f32),
            pltpu.VMEM((convs, rims, SIDE, inner), f32),
            pltpu.VMEM((SIDE + 2, 2 * SIDE, width + 2 * pair), f32),
            pltpu.VMEM((SIDE + 2, group * 2 * SIDE, 2 * kdy), bf16),
            pltpu.VMEM((3, 2 * kdy, half), bf16),
            pltpu.VMEM((3, kdy, half), bf16),
            pltpu.VMEM((convs, taps, rows, pair), f32),
            pltpu.VMEM((4, ch, pair), f32),
            pltpu.VMEM((SIDE, group * 2 * SIDE, half), f32),
            pltpu.SMEM((entries,), jnp.int32),
            pltpu.SMEM((bricks,), jnp.int32),
            pltpu.SMEM((bricks,), jnp.int32),
            pltpu.SMEM(neighbours.shape, jnp.int32),
            pltpu.SemaphoreType.DMA((convs,)),
            pltpu.SemaphoreType.DMA((convs, 4, 3 * rims)),
            pltpu.SemaphoreType.DMA((convs, 4, 3 * rims)),
        ]
        + [pltpu.VMEM((entries, 2, SIDE, width), f32) for _ in range(2 * convs)]
        + [pltpu.VMEM((entries, SIDE, inner), f32) for _ in range(convs)],
        compiler_params=pltpu.CompilerParams(
            collective_id=0, has_side_effects=True, vmem_limit_bytes=56 * 1024 * 1024
        ),
        name="layers",
    )(neighbours, live, rim_slots, features, biases, planes)


def solution(mesh):
    in_specs = (
        P(("space", "slab"), None, None, None),
        P(("space", "slab")),
        P(("space", "slab"), None),
        P(("space", "slab"), None),
        P(),
        P(),
    )
    out_specs = P(("space", "slab"), None, None, None)
    body = functools.partial(shards, mesh.shape["space"], mesh.shape["slab"])
    return jax.shard_map(body, mesh=mesh, in_specs=in_specs, out_specs=out_specs, check_vma=False)
```

time: 75.2 us -> 51.8 us (0.69)
  Pallas kernels: 68.3 us -> 49.1 us
  local copies, waits for them, and re-layouts: 6.04 us -> 1.87 us
    pallas_call x1, Pallas kernels: 68.3 us -> 49.1 us  [shards(): pl.pallas_call(functools.partial(layers_kernel, nsp, nsl), out_shape=jax....]
    reshape x1 -> x0, local copies, waits for them, and re-layouts: 4.18 us -> none  [shards(): taps = weights.transpose(1, 0, 2).reshape(weights.shape[1], convs, ch, ch)]
where the time goes in v1:
time: 51.8 us; the launch traced here: 51.6 us
  Pallas kernels  49.1 us (95%)
  local copies, waits for them, and re-layouts  1.87 us (4%)
  between operations  0.66 us (1%)
    pallas_call x1, Pallas kernels, shards(): pl.pallas_call(functools.partial(layers_kernel, nsp, nsl), out_shape=jax....  49.1 us
    unnamed x1, local copies, waits for them, and re-layouts  1.87 us

profile of v1, /device:TPU:12, one launch (start us, length us, event | category | flops | bytes accessed | tf_op | source)
XLA Modules:
  0.0 51.6 jit_solution(13017612564390608230)
XLA Ops:
  0.7 49.1 %layers.1 = f32[4,8,8,512]{3,2,1,0:T(8,128)} custom-call(s32[4,26]{1,0:T(4,128)} %nbr.1, s32[1]{0:T(128)S(6)} %copy.8.live, s32[1,2]{1,0:T(1,128)} %rim.1, f32[4,8,8,512]{3,2,1,0:T(8,128)} %feat.1, f32[4,64]{1,0:T(4,128)} %bias.1, f32[27,32,4,128]{3,2,1,0:T(4,128)} %bitcast.3), custom_call_target="tpu_custom_call" | custom-call | tf_op jit(solution)/shard_map/layers/pallas_call | solution.py:447
  49.7 1.9 %copy.9 = f32[4,8,8,512]{3,2,1,0:T(8,128)} copy(f32[4,8,8,512]{3,2,1,0:T(8,128)} %layers.1) | data formatting | bytes 1048576

commit v2 on v1

v2 whole, which is shorter than its diff:
```python
import functools

import jax
import jax.numpy as jnp
from jax import lax
from jax.experimental import pallas as pl
from jax.experimental.pallas import tpu as pltpu
from jax.sharding import PartitionSpec as P

MESH = pl.DeviceIdType.MESH
SIDE = 8
RELAYED = (3, 3)


def direction_number(dx, dy, dz):
    index = 9 * (dx + 1) + 3 * (dy + 1) + (dz + 1)
    return index if index < 13 else index - 1


def layers_kernel(
    nsp, nsl, nbr, live, rim, f_hbm, b_hbm, w_hbm, out,
    feat, bias, cur, hid, stage, offx, offy, offz, pad, cols, whi, wlo, wbuf, blk, acc,
    emap, inv, perm, nb, isem, osem, wsem, ssem, rsem, *tabs,
):
    bricks = f_hbm.shape[0]
    width = f_hbm.shape[-1]
    ch = width // SIDE
    half = width // 2
    pair = 2 * ch
    ktile = half + pair
    kdy = 3 * ktile
    rims = rim.shape[1]
    convs = w_hbm.shape[2]
    tabx, taby, tabz = tabs[:convs], tabs[convs:2 * convs], tabs[2 * convs:]
    last = bricks + 4 * rims
    sp = lax.axis_index("space")
    sl = lax.axis_index("slab")
    odd = lax.rem(sp, 2)

    near = (sp + 1 - 2 * odd, sl)
    far = (sp - 1 + 2 * odd, sl)
    via = (sp - 2 + 4 * odd, sl)
    onto = (sp + 2 - 4 * odd, sl)
    has_far = jnp.where(odd == 1, sp < nsp - 1, sp > 0)
    has_onto = jnp.where(odd == 1, sp > 1, sp < nsp - 2)
    lower = (sl > 0, (sp, sl - 1))
    upper = (sl < nsl - 1, (sp, sl + 1))
    near_first = bricks + rims * (1 - odd)
    far_first = bricks + rims * odd

    barrier = pltpu.get_barrier_semaphore()
    greeted = ((sp >= 0, near), (has_far, far), (has_far, via), (has_onto, onto), lower, upper)
    for has, peer in greeted:
        @pl.when(has)
        def _():
            pl.semaphore_signal(barrier, inc=1, device_id=peer, device_id_type=MESH)

    def weight_copy(k):
        return pltpu.make_async_copy(w_hbm.at[:, :, k], wbuf.at[k], wsem.at[k])

    feature_copy = pltpu.make_async_copy(f_hbm, feat, isem.at[0])
    bias_copy = pltpu.make_async_copy(b_hbm, bias, isem.at[1])
    feature_copy.start()
    bias_copy.start()
    for k in range(convs):
        weight_copy(k).start()

    def out_copy(b):
        return pltpu.make_async_copy(stage.at[b], out.at[b], osem.at[b])

    chunks = [(j, part) for j in range(rims) for part in range(3)]
    relayed = [min(RELAYED[min(k, 1)], len(chunks)) for k in range(convs)]

    def offered(k, j, part):
        if j == 0:
            return entry_of(k, 0, part)
        if part == 0:
            return offx.at[k, j - 1]
        if part == 1:
            return offy.at[k, j - 1, :, 1:SIDE - 1, :]
        return offz.at[k, j - 1]

    def entry_of(k, at, part):
        if part == 0:
            return tabx[k].at[at]
        if part == 1:
            return taby[k].at[at, :, 1:SIDE - 1, :]
        return tabz[k].at[at]

    def copy(k, src, dst, flow, index, peer):
        return pltpu.make_async_remote_copy(
            src_ref=src, dst_ref=dst, send_sem=ssem.at[k, flow, index],
            recv_sem=rsem.at[k, flow, index], device_id=peer, device_id_type=MESH,
        )

    def to_near(k, c):
        j, part = chunks[c]
        return copy(k, offered(k, j, part), entry_of(k, far_first + j, part), 0, c, near)

    def from_near(k, c):
        j, part = chunks[c]
        return copy(k, offered(k, j, part), entry_of(k, near_first + j, part), 0, c, near)

    def to_far(k, c):
        j, part = chunks[c]
        return copy(k, offered(k, j, part), entry_of(k, near_first + j, part), 1, c, far)

    def relay(k, c):
        j, part = chunks[c]
        return copy(
            k, entry_of(k, near_first + j, part), entry_of(k, far_first + j, part), 1, c, onto
        )

    def from_far(k, c):
        j, part = chunks[c]
        return copy(k, offered(k, j, part), entry_of(k, far_first + j, part), 1, c, far)

    def beside(k, d, j, part, to):
        first = bricks + rims * (d ^ 1 if to else d)
        index = 3 * j + part
        peer = (lower if d == 2 else upper)[1]
        return pltpu.make_async_remote_copy(
            src_ref=offered(k, j, part), dst_ref=entry_of(k, first + j, part),
            send_sem=ssem.at[k, d, index], recv_sem=rsem.at[k, d ^ 1 if to else d, index],
            device_id=peer, device_id_type=MESH,
        )

    def send(k, brick):
        own = range(3 * brick, 3 * brick + 3)
        for c in own:
            if c < relayed[k]:
                to_near(k, c).start()

        for c in own:
            if c >= relayed[k]:
                to_near(k, c).start()

                @pl.when(has_far)
                def _():
                    to_far(k, c).start()
        for d, (has, _) in ((2, lower), (3, upper)):
            @pl.when(has)
            def _():
                for part in range(3):
                    beside(k, d, brick, part, True).start()

    def pass_on(k, some):
        for c in some:
            from_near(k, c).wait_recv()

            @pl.when(has_onto)
            def _():
                relay(k, c).start()

    def receive(k):
        for c in range(relayed[k], len(chunks)):
            from_near(k, c).wait_recv()
        for d, (has, _) in ((2, lower), (3, upper)):
            @pl.when(has)
            def _():
                for j, part in chunks:
                    beside(k, d, j, part, False).wait_recv()

        @pl.when(has_far)
        def _():
            for c in range(len(chunks)):
                from_far(k, c).wait_recv()

    def finish_sends(k):
        for c in range(len(chunks)):
            to_near(k, c).wait_send()

        @pl.when(has_far)
        def _():
            for c in range(relayed[k], len(chunks)):
                to_far(k, c).wait_send()

        @pl.when(has_onto)
        def _():
            for c in range(relayed[k]):
                relay(k, c).wait_send()
        for d, (has, _) in ((2, lower), (3, upper)):
            @pl.when(has)
            def _():
                for j, part in chunks:
                    beside(k, d, j, part, True).wait_send()

    slots = [rim[0, j] for j in range(rims)]
    score = []
    for b in range(bricks):
        s = rims + b
        for j in reversed(range(rims)):
            s = jnp.where(slots[j] == b, j, s)
        score.append(s)
    place = [
        sum(jnp.where(score[o] < score[b], 1, 0) for o in range(bricks) if o != b)
        for b in range(bricks)
    ]
    held = [
        sum(jnp.where(place[b] == p, b, 0) for b in range(bricks)) for p in range(bricks)
    ]
    for b in range(bricks):
        inv[b] = place[b]
        perm[b] = held[b]
    spot = [sum(jnp.where(slots[j] == b, place[b], 0) for b in range(bricks)) for j in range(rims)]

    def mask_of(b):
        return jnp.where(b < live[0, 0], 1.0, 0.0).astype(jnp.float32)

    low = lax.broadcasted_iota(jnp.int32, (SIDE, pair), 1) < ch
    low1 = lax.broadcasted_iota(jnp.int32, (1, pair), 1) < ch
    loww = lax.broadcasted_iota(jnp.int32, wbuf.shape[2:], 1) < ch

    def take_faces(src, k, p):
        tabx[k][p, 0] = src[p, 0]
        tabx[k][p, 1] = src[p, SIDE - 1]
        for s, y in ((0, 0), (1, SIDE - 1)):
            for x in range(1, SIDE - 1):
                taby[k][p, s, x:x + 1, :] = src[p, x, y:y + 1, :]
        for x in range(1, SIDE - 1):
            at = (x - 1) * pair
            tabz[k][p, :, at:at + pair] = jnp.where(
                low, src[p, x, :, 0:pair], src[p, x, :, width - pair:width]
            )

    def offer(k, j):
        if j > 0:
            for off, tab in ((offx, tabx[k]), (offy, taby[k]), (offz, tabz[k])):
                value = tab[0]
                for p in range(1, j + 1):
                    value = jnp.where(spot[j] == p, tab[p], value)
                off[k, j - 1] = value
        send(k, j)

    def build_weights(k):
        weight_copy(k).wait()
        w = k % 2

        def one(t, carry):
            a = t // 3
            base = pl.multiple_of((t - 3 * a) * ktile, ktile)
            taps = [wbuf[k, 3 * t + i] for i in range(3)]
            turned = [pltpu.roll(tap, ch, 1) for tap in taps]
            none = jnp.zeros(taps[0].shape, jnp.float32)
            rows = taps[0].shape[0]
            for j in range(4):
                first, first_turned = (taps[j], turned[j]) if j < 3 else (none, none)
                second, second_turned = (taps[j - 1], turned[j - 1]) if j > 0 else (none, none)
                blk[j, pl.ds(0, rows, stride=2), :] = jnp.where(loww, first, second_turned)
                blk[j, pl.ds(1, rows, stride=2), :] = jnp.where(loww, first_turned, second)
            for j in range(4):
                block = blk[j]
                hi = block.astype(jnp.bfloat16)
                lo = (block - hi.astype(jnp.float32)).astype(jnp.bfloat16)
                for q in range(2):
                    z = j - 1 + 2 * q
                    row = base + (z if z >= 0 else 5) * ch
                    row = pl.multiple_of(row, ch)
                    lanes = slice(q * pair, (q + 1) * pair)
                    whi[w, a, pl.ds(row, ch), lanes] = hi
                    whi[w, a, pl.ds(pl.multiple_of(row + kdy, ch), ch), lanes] = hi
                    wlo[w, a, pl.ds(row, ch), lanes] = lo
            return carry

        lax.fori_loop(0, 9, one, 0)

    def row_of(center, below, above, mask):
        return jnp.concatenate(
            [
                center[:, :half],
                jnp.where(mask, center[:, half:half + pair], below),
                center[:, half:],
                jnp.where(mask, above, center[:, half - pair:half]),
            ],
            axis=1,
        )

    def build_columns(src, k, p, c):
        tx, ty, tz = tabx[k], taby[k], tabz[k]

        def entry(dx, dy, dz):
            return nb[p, direction_number(dx, dy, dz)]

        def x_row(dx, dy, s, y):
            return row_of(
                tx[entry(dx, dy, 0), s, y:y + 1, :],
                tx[entry(dx, dy, -1), s, y:y + 1, width - pair:width],
                tx[entry(dx, dy, 1), s, y:y + 1, 0:pair],
                low1,
            )

        for dx, xrow, s in ((-1, 0, 1), (1, SIDE + 1, 0)):
            pad[xrow, 1:SIDE + 1, :] = row_of(
                tx[entry(dx, 0, 0), s],
                tx[entry(dx, 0, -1), s, :, width - pair:width],
                tx[entry(dx, 0, 1), s, :, 0:pair],
                low,
            )
            for dy, yrow, y in ((-1, 0, SIDE - 1), (1, SIDE + 1, 0)):
                pad[xrow, yrow:yrow + 1, :] = x_row(dx, dy, s, y)
        nlow, nhigh = entry(0, 0, -1), entry(0, 0, 1)
        for x in range(SIDE):
            if x in (0, SIDE - 1):
                s = 0 if x == 0 else 1
                below = tx[nlow, s, :, width - pair:width]
                above = tx[nhigh, s, :, 0:pair]
            else:
                at = (x - 1) * pair
                below = tz[nlow, :, at:at + pair]
                above = tz[nhigh, :, at:at + pair]
            pad[1 + x, 1:SIDE + 1, :] = row_of(src[p, x], below, above, low)
        for dy, yrow, s, y in ((-1, 0, 1, SIDE - 1), (1, SIDE + 1, 0, 0)):
            rows = row_of(
                ty[entry(0, dy, 0), s],
                ty[entry(0, dy, -1), s, :, width - pair:width],
                ty[entry(0, dy, 1), s, :, 0:pair],
                low,
            )
            for x in range(1, SIDE - 1):
                pad[1 + x, yrow:yrow + 1, :] = rows[x:x + 1]
            pad[1, yrow:yrow + 1, :] = x_row(0, dy, 0, y)
            pad[SIDE, yrow:yrow + 1, :] = x_row(0, dy, 1, y)
        for x in range(SIDE + 2):
            for dy in range(3):
                v = pad[x, dy:dy + SIDE, :]
                v = jnp.concatenate([v[:, :ktile], v[:, ktile:]], axis=0)
                hi = v.astype(jnp.bfloat16)
                lo = (v - hi.astype(jnp.float32)).astype(jnp.bfloat16)
                cols[c, x, :, dy * ktile:(dy + 1) * ktile] = hi
                cols[c, x, :, kdy + dy * ktile:kdy + (dy + 1) * ktile] = lo

    def convolve(k, c):
        w = k % 2
        rows = SIDE * 2 * SIDE
        left = [cols[c, a:a + SIDE].reshape(rows, 2 * kdy) for a in range(3)]

        def dot(x, y):
            return jnp.dot(x, y, preferred_element_type=jnp.float32)

        tile = 2 * pair
        tiles = -(-2 * kdy // tile) + -(-kdy // tile)
        cut = (tiles // 2) * tile
        one = dot(left[0], whi[w, 0]) + dot(left[0][:, :kdy], wlo[w, 0])
        one = one + dot(left[1][:, :cut], whi[w, 1, :cut])
        two = dot(left[2], whi[w, 2]) + dot(left[2][:, :kdy], wlo[w, 2])
        two = two + dot(left[1][:, cut:], whi[w, 1, cut:]) + dot(left[1][:, :kdy], wlo[w, 1])
        acc[odd] = one
        acc[1 - odd] = two

    def epilogue(k, res, dst, p, at, m):
        bvec = bias[k:k + 1, :]
        bvec = jnp.concatenate([bvec, bvec, bvec, bvec], axis=1)
        for x in range(SIDE):
            for t in range(2):
                row = (2 * x + t) * SIDE
                v = acc[0, row:row + SIDE, :] + acc[1, row:row + SIDE, :] + bvec
                lanes = slice(t * half, (t + 1) * half)
                if res is not None:
                    v = v + res[p, x, :, lanes]
                dst[at, x, :, lanes] = jnp.maximum(v, 0.0) * m

    def mask_features(p, carry):
        cur[p] = feat[perm[p]] * mask_of(perm[p])
        return carry

    feature_copy.wait()
    lax.fori_loop(0, bricks, mask_features, 0)
    for p in range(rims):
        take_faces(cur, 0, p)
    arrivals = sum(jnp.where(has, 1, 0) for has, _ in greeted)
    pl.semaphore_wait(barrier, arrivals)
    for j in range(rims):
        offer(0, j)

    for p in range(rims, bricks):
        take_faces(cur, 0, p)
    for k in range(convs):
        for tab in (tabx[k], taby[k], tabz[k]):
            tab[last] = jnp.zeros(tab.shape[1:], jnp.float32)
    for e in range(last + 1):
        if e < bricks:
            emap[e] = place[e]
        elif e < bricks + rims:
            emap[e] = jnp.where(sp > 0, e, last)
        elif e < bricks + 2 * rims:
            emap[e] = jnp.where(sp < nsp - 1, e, last)
        elif e < bricks + 3 * rims:
            emap[e] = jnp.where(sl > 0, e, last)
        elif e < last:
            emap[e] = jnp.where(sl < nsl - 1, e, last)
        else:
            emap[e] = last

    def remap(j, carry):
        for p in range(bricks):
            nb[p, j] = emap[nbr[perm[p], j]]
        return carry

    lax.fori_loop(0, nbr.shape[1], remap, 0)
    whi[...] = jnp.zeros_like(whi)
    wlo[...] = jnp.zeros_like(wlo)
    build_weights(0)
    bias_copy.wait()
    pass_on(0, range(relayed[0]))

    for k in range(convs):
        src = cur if k % 2 == 0 else hid
        res = None if k % 2 == 0 else cur
        receive(k)
        end = k == convs - 1
        if end:
            dst = stage
            spots = [inv[b] for b in range(bricks)]
        else:
            dst = hid if k % 2 == 0 else cur
            spots = list(range(bricks))
        waiting = [] if end else list(range(relayed[k + 1]))
        build_columns(src, k, spots[0], 0)
        for i in range(bricks):
            p = spots[i]
            if i + 1 < bricks and (end or i != 0):
                build_columns(src, k, spots[i + 1], (i + 1) % 2)
            convolve(k, i % 2)
            if end:
                epilogue(k, res, dst, p, i, mask_of(i))
                out_copy(i).start()
                continue
            epilogue(k, res, dst, p, i, mask_of(perm[i]))
            take_faces(dst, k + 1, i)
            if i < rims:
                offer(k + 1, i)
                if i == 0 and bricks > 1:
                    build_columns(src, k, spots[1], 1)
            elif i == rims:
                pass_on(k + 1, waiting[:1])
                build_weights(k + 1)
                pass_on(k + 1, waiting[1:3])
                waiting = waiting[3:]
        if not end:
            pass_on(k + 1, waiting)
    for b in range(bricks):
        out_copy(b).wait()
    for k in range(convs):
        finish_sends(k)


def shards(nsp, nsl, features, live, rim_slots, neighbours, weights, biases):
    bricks, _, _, width = features.shape
    ch = biases.shape[-1]
    convs, taps, _ = weights.shape
    rims = rim_slots.shape[-1]
    entries = bricks + 4 * rims + 1
    pair = 2 * ch
    rows = ch * ch // pair
    planes = weights.reshape(convs, taps, rows, pair).transpose(1, 2, 0, 3)
    half = width // 2
    kdy = 3 * (half + pair)
    inner = (SIDE - 2) * pair
    f32, bf16 = jnp.float32, jnp.bfloat16
    smem = pl.BlockSpec(memory_space=pltpu.SMEM)
    hbm = pl.BlockSpec(memory_space=pl.ANY)
    return pl.pallas_call(
        functools.partial(layers_kernel, nsp, nsl),
        out_shape=jax.ShapeDtypeStruct(features.shape, f32),
        in_specs=[smem, smem, smem, hbm, hbm, hbm],
        out_specs=hbm,
        scratch_shapes=[
            pltpu.VMEM(features.shape, f32),
            pltpu.VMEM(biases.shape, f32),
            pltpu.VMEM(features.shape, f32),
            pltpu.VMEM(features.shape, f32),
            pltpu.VMEM(features.shape, f32),
            pltpu.VMEM((convs, max(rims - 1, 1), 2, SIDE, width), f32),
            pltpu.VMEM((convs, max(rims - 1, 1), 2, SIDE, width), f32),
            pltpu.VMEM((convs, max(rims - 1, 1), SIDE, inner), f32),
            pltpu.VMEM((SIDE + 2, 2 * SIDE, width + 2 * pair), f32),
            pltpu.VMEM((2, SIDE + 2, 2 * SIDE, 2 * kdy), bf16),
            pltpu.VMEM((2, 3, 2 * kdy, half), bf16),
            pltpu.VMEM((2, 3, kdy, half), bf16),
            pltpu.VMEM((convs, taps, rows, pair), f32),
            pltpu.VMEM((4, ch, pair), f32),
            pltpu.VMEM((2, SIDE * 2 * SIDE, half), f32),
            pltpu.SMEM((entries,), jnp.int32),
            pltpu.SMEM((bricks,), jnp.int32),
            pltpu.SMEM((bricks,), jnp.int32),
            pltpu.SMEM(neighbours.shape, jnp.int32),
            pltpu.SemaphoreType.DMA((2,)),
            pltpu.SemaphoreType.DMA((bricks,)),
            pltpu.SemaphoreType.DMA((convs,)),
            pltpu.SemaphoreType.DMA((convs, 4, 3 * rims)),
            pltpu.SemaphoreType.DMA((convs, 4, 3 * rims)),
        ]
        + [pltpu.VMEM((entries, 2, SIDE, width), f32) for _ in range(2 * convs)]
        + [pltpu.VMEM((entries, SIDE, inner), f32) for _ in range(convs)],
        compiler_params=pltpu.CompilerParams(
            collective_id=0, has_side_effects=True, vmem_limit_bytes=56 * 1024 * 1024
        ),
        name="layers",
    )(neighbours, live.reshape(1, 1), rim_slots, features, biases, planes)


def solution(mesh):
    in_specs = (
        P(("space", "slab"), None, None, None),
        P(("space", "slab")),
        P(("space", "slab"), None),
        P(("space", "slab"), None),
        P(),
        P(),
    )
    out_specs = P(("space", "slab"), None, None, None)
    body = functools.partial(shards, mesh.shape["space"], mesh.shape["slab"])
    return jax.shard_map(body, mesh=mesh, in_specs=in_specs, out_specs=out_specs, check_vma=False)
```

time: 51.8 us -> 46.3 us (0.89); the launches traced: 51.6 us -> 45.4 us
  Pallas kernels: 49.1 us -> 42.9 us
    pallas_call x1, Pallas kernels: 49.1 us -> 42.9 us  [shards(): pl.pallas_call(functools.partial(layers_kernel, nsp, nsl), out_shape=jax....]
where the time goes in v2:
time: 46.3 us; the launch traced here: 45.4 us
  Pallas kernels  42.9 us (93%)
  local copies, waits for them, and re-layouts  1.87 us (4%)
  between operations  0.66 us (1%)
    pallas_call x1, Pallas kernels, shards(): pl.pallas_call(functools.partial(layers_kernel, nsp, nsl), out_shape=jax....  42.9 us
    unnamed x1, local copies, waits for them, and re-layouts  1.87 us

profile of v2, /device:TPU:12, one launch (start us, length us, event | category | flops | bytes accessed | tf_op | source)
XLA Modules:
  0.0 45.4 jit_solution(6708197351201559952)
XLA Ops:
  0.7 42.9 %layers.1 = f32[4,8,8,512]{3,2,1,0:T(8,128)} custom-call(s32[4,26]{1,0:T(4,128)} %nbr.1, s32[1,1]{1,0:T(1,128)} %bitcast.4.live, s32[1,2]{1,0:T(1,128)} %rim.1, f32[4,8,8,512]{3,2,1,0:T(8,128)} %f_hbm.1, f32[4,64]{1,0:T(4,128)} %b_hbm.1, f32[27,32,4,128]{3,2,1,0:T(4,128)} %bitcast.5), custom_call_target="tpu_custom_call" | custom-call | tf_op jit(solution)/shard_map/layers/pallas_call | solution.py:462
  43.5 1.9 %copy.9 = f32[4,8,8,512]{3,2,1,0:T(8,128)} copy(f32[4,8,8,512]{3,2,1,0:T(8,128)} %layers.1) | data formatting | bytes 1048576

commit v3 on v2

--- a/solution.py
+++ b/solution.py
@@ -18,9 +18,9 @@
 
 
 def layers_kernel(
-    nsp, nsl, nbr, live, rim, f_hbm, b_hbm, w_hbm, out,
+    nsp, nsl, nbr_hbm, live_hbm, rim_hbm, f_hbm, b_hbm, w_hbm, out,
     feat, bias, cur, hid, stage, offx, offy, offz, pad, cols, whi, wlo, wbuf, blk, acc,
-    emap, inv, perm, nb, isem, osem, wsem, ssem, rsem, *tabs,
+    nbr, live, rim, emap, inv, perm, nb, isem, osem, wsem, ssem, rsem, *tabs,
 ):
     bricks = f_hbm.shape[0]
     width = f_hbm.shape[-1]
@@ -29,7 +29,7 @@
     pair = 2 * ch
     ktile = half + pair
     kdy = 3 * ktile
-    rims = rim.shape[1]
+    rims = rim_hbm.shape[1]
     convs = w_hbm.shape[2]
     tabx, taby, tabz = tabs[:convs], tabs[convs:2 * convs], tabs[2 * convs:]
     last = bricks + 4 * rims
@@ -60,7 +60,13 @@
 
     feature_copy = pltpu.make_async_copy(f_hbm, feat, isem.at[0])
     bias_copy = pltpu.make_async_copy(b_hbm, bias, isem.at[1])
+    index_copies = [
+        pltpu.make_async_copy(a, b, isem.at[2 + i])
+        for i, (a, b) in enumerate(((rim_hbm, rim), (live_hbm, live), (nbr_hbm, nbr)))
+    ]
     feature_copy.start()
+    for index_copy in index_copies:
+        index_copy.start()
     bias_copy.start()
     for k in range(convs):
         weight_copy(k).start()
@@ -78,14 +84,14 @@
             return offx.at[k, j - 1]
         if part == 1:
             return offy.at[k, j - 1, :, 1:SIDE - 1, :]
-        return offz.at[k, j - 1]
+        return offz.at[k, j - 1, 1:SIDE - 1, :]
 
     def entry_of(k, at, part):
         if part == 0:
             return tabx[k].at[at]
         if part == 1:
             return taby[k].at[at, :, 1:SIDE - 1, :]
-        return tabz[k].at[at]
+        return tabz[k].at[at, 1:SIDE - 1, :]
 
     def copy(k, src, dst, flow, index, peer):
         return pltpu.make_async_remote_copy(
@@ -184,6 +190,9 @@
             def _():
                 for j, part in chunks:
                     beside(k, d, j, part, True).wait_send()
+
+    for index_copy in index_copies:
+        index_copy.wait()
 
     slots = [rim[0, j] for j in range(rims)]
     score = []
@@ -205,7 +214,7 @@
     spot = [sum(jnp.where(slots[j] == b, place[b], 0) for b in range(bricks)) for j in range(rims)]
 
     def mask_of(b):
-        return jnp.where(b < live[0, 0], 1.0, 0.0).astype(jnp.float32)
+        return jnp.where(b < live[0], 1.0, 0.0).astype(jnp.float32)
 
     low = lax.broadcasted_iota(jnp.int32, (SIDE, pair), 1) < ch
     low1 = lax.broadcasted_iota(jnp.int32, (1, pair), 1) < ch
@@ -309,6 +318,17 @@
                 below = tz[nlow, :, at:at + pair]
                 above = tz[nhigh, :, at:at + pair]
             pad[1 + x, 1:SIDE + 1, :] = row_of(src[p, x], below, above, low)
+            if 0 < x < SIDE - 1:
+                for s, y in ((0, 0), (1, SIDE - 1)):
+                    row = slice(1 + y, 2 + y)
+                    pad[1 + x, row, half:half + pair] = jnp.where(
+                        low1, src[p, x, y:y + 1, half:half + pair],
+                        ty[nlow, s, x:x + 1, width - pair:width],
+                    )
+                    pad[1 + x, row, width + pair:width + 2 * pair] = jnp.where(
+                        low1, ty[nhigh, s, x:x + 1, 0:pair],
+                        src[p, x, y:y + 1, half - pair:half],
+                    )
         for dy, yrow, s, y in ((-1, 0, 1, SIDE - 1), (1, SIDE + 1, 0, 0)):
             rows = row_of(
                 ty[entry(0, dy, 0), s],
@@ -457,13 +477,15 @@
     kdy = 3 * (half + pair)
     inner = (SIDE - 2) * pair
     f32, bf16 = jnp.float32, jnp.bfloat16
-    smem = pl.BlockSpec(memory_space=pltpu.SMEM)
-    hbm = pl.BlockSpec(memory_space=pl.ANY)
+    hbm = pl.BlockSpec(memory_space=pltpu.HBM)
+    def far(a):
+        return pltpu.with_memory_space_constraint(a, pltpu.HBM)
+
     return pl.pallas_call(
         functools.partial(layers_kernel, nsp, nsl),
         out_shape=jax.ShapeDtypeStruct(features.shape, f32),
-        in_specs=[smem, smem, smem, hbm, hbm, hbm],
-        out_specs=hbm,
+        in_specs=[hbm] * 6,
+        out_specs=pl.BlockSpec(memory_space=pl.ANY),
         scratch_shapes=[
             pltpu.VMEM(features.shape, f32),
             pltpu.VMEM(biases.shape, f32),
@@ -480,11 +502,14 @@
             pltpu.VMEM((convs, taps, rows, pair), f32),
             pltpu.VMEM((4, ch, pair), f32),
             pltpu.VMEM((2, SIDE * 2 * SIDE, half), f32),
+            pltpu.SMEM(neighbours.shape, jnp.int32),
+            pltpu.SMEM(live.shape, jnp.int32),
+            pltpu.SMEM(rim_slots.shape, jnp.int32),
             pltpu.SMEM((entries,), jnp.int32),
             pltpu.SMEM((bricks,), jnp.int32),
             pltpu.SMEM((bricks,), jnp.int32),
             pltpu.SMEM(neighbours.shape, jnp.int32),
-            pltpu.SemaphoreType.DMA((2,)),
+            pltpu.SemaphoreType.DMA((5,)),
             pltpu.SemaphoreType.DMA((bricks,)),
             pltpu.SemaphoreType.DMA((convs,)),
             pltpu.SemaphoreType.DMA((convs, 4, 3 * rims)),
@@ -493,10 +518,10 @@
         + [pltpu.VMEM((entries, 2, SIDE, width), f32) for _ in range(2 * convs)]
         + [pltpu.VMEM((entries, SIDE, inner), f32) for _ in range(convs)],
         compiler_params=pltpu.CompilerParams(
-            collective_id=0, has_side_effects=True, vmem_limit_bytes=56 * 1024 * 1024
+            collective_id=0, has_side_effects=True, vmem_limit_bytes=26 * 1024 * 1024
         ),
         name="layers",
-    )(neighbours, live.reshape(1, 1), rim_slots, features, biases, planes)
+    )(far(neighbours), live, far(rim_slots), far(features), far(biases), far(planes))
 
 
 def solution(mesh):

time: 46.3 us -> 44.6 us (0.963)
  local copies, waits for them, and re-layouts: 1.87 us -> 0.8 us
    unnamed x1, local copies, waits for them, and re-layouts: 1.87 us -> 0.8 us
where the time goes in v3:
time: 44.6 us; the launch traced here: 44 us
  Pallas kernels  42.6 us (96%)
  local copies, waits for them, and re-layouts  0.8 us (2%)
  between operations  0.66 us (1%)
    pallas_call x1, Pallas kernels, shards(): pl.pallas_call(functools.partial(layers_kernel, nsp, nsl), out_shape=jax....  42.6 us

profile of v3, /device:TPU:12, one launch (start us, length us, event | category | flops | bytes accessed | tf_op | source)
XLA Modules:
  0.0 44.0 jit_solution(157854516920975011)
XLA Ops:
  0.7 42.6 %layers.1 = f32[4,8,8,512]{3,2,1,0:T(8,128)S(1)} custom-call(s32[4,26]{1,0:T(4,128)} %nbr_hbm.1, s32[1]{0:T(128)S(6)} %copy.8.live_hbm, s32[1,2]{1,0:T(1,128)} %rim_hbm.1, f32[4,8,8,512]{3,2,1,0:T(8,128)} %f_hbm.1, f32[4,64]{1,0:T(4,128)} %b_hbm.1, f32[27,32,4,128]{3,2,1,0:T(4,128)} %bitcast.3), custom_call_target="tpu_custom_call" | custom-call | tf_op jit(solution)/shard_map/layers/pallas_call | solution.py:484
  43.2 0.8 %copy.9 = f32[4,8,8,512]{3,2,1,0:T(8,128)} copy(f32[4,8,8,512]{3,2,1,0:T(8,128)S(1)} %layers.1) | data formatting | bytes 1048576

commit v4 on v3

--- a/solution.py
+++ b/solution.py
@@ -9,7 +9,7 @@
 
 MESH = pl.DeviceIdType.MESH
 SIDE = 8
-RELAYED = (3, 3)
+RELAYED = (3, 2)
 
 
 def direction_number(dx, dy, dz):
@@ -451,13 +451,9 @@
                 offer(k + 1, i)
                 if i == 0 and bricks > 1:
                     build_columns(src, k, spots[1], 1)
-            elif i == rims:
-                pass_on(k + 1, waiting[:1])
-                build_weights(k + 1)
-                pass_on(k + 1, waiting[1:3])
-                waiting = waiting[3:]
         if not end:
             pass_on(k + 1, waiting)
+            build_weights(k + 1)
     for b in range(bricks):
         out_copy(b).wait()
     for k in range(convs):

time: 44.6 us -> 43.2 us (0.969)
  Pallas kernels: 42.6 us -> 41.1 us
    pallas_call x1, Pallas kernels: 42.6 us -> 41.1 us  [shards(): pl.pallas_call(functools.partial(layers_kernel, nsp, nsl), out_shape=jax....]
where the time goes in v4:
time: 43.2 us; the launch traced here: 42.6 us
  Pallas kernels  41.1 us (95%)
  local copies, waits for them, and re-layouts  0.8 us (2%)
  between operations  0.66 us (2%)
    pallas_call x1, Pallas kernels, shards(): pl.pallas_call(functools.partial(layers_kernel, nsp, nsl), out_shape=jax....  41.1 us

profile of v4, /device:TPU:12, one launch (start us, length us, event | category | flops | bytes accessed | tf_op | source)
XLA Modules:
  0.0 42.6 jit_solution(1996735429091453133)
XLA Ops:
  0.7 41.1 %layers.1 = f32[4,8,8,512]{3,2,1,0:T(8,128)S(1)} custom-call(s32[4,26]{1,0:T(4,128)} %nbr_hbm.1, s32[1]{0:T(128)S(6)} %copy.8.live_hbm, s32[1,2]{1,0:T(1,128)} %rim_hbm.1, f32[4,8,8,512]{3,2,1,0:T(8,128)} %f_hbm.1, f32[4,64]{1,0:T(4,128)} %b_hbm.1, f32[27,32,4,128]{3,2,1,0:T(4,128)} %bitcast.3), custom_call_target="tpu_custom_call" | custom-call | tf_op jit(solution)/shard_map/layers/pallas_call | solution.py:480
  41.8 0.8 %copy.9 = f32[4,8,8,512]{3,2,1,0:T(8,128)} copy(f32[4,8,8,512]{3,2,1,0:T(8,128)S(1)} %layers.1) | data formatting | bytes 1048576
